TPU v7x, 256 devices: a whole 4x4x8 slice. The times are simulated.
256 devices in a mesh: grp: 8 (over y, core), sub: 32 (over z, x).
Axes of the slice: x: 4, y: 4, z: 8, core: 2. Of those that a mesh axis runs over, the one named last changes fastest.
Arguments:
- iterate: bfloat16 [262144, 1024], P(('grp', 'sub')), may hold values from -6 to 6
- load: bfloat16 [262144, 1024], P(('grp', 'sub')), may hold values from -6 to 6
- schur: bfloat16 [262144, 1024], P(('grp', 'sub'))
- local_inverse: bfloat16 [262144, 1024], P(('grp', 'sub'))
- basis: bfloat16 [6144, 1024], P(('grp', 'sub')), may hold values from -0.1875 to 0.1875
- coarse_inverse: float32 [1024, 1024], P('grp')
- owner: int32 [256, 24], P(('grp', 'sub')), may hold values from 0 to 1023, as said below
- shared_index: int32 [256, 6, 224], P(('grp', 'sub')), may hold values from 0 to 1023, as said below
- shared_count: int32 [256, 6], P(('grp', 'sub')), may hold values from 179 to 224, as said below
Outputs:
- new_iterate: bfloat16 [262144, 1024], P(('grp', 'sub'))
- residual: bfloat16 [262144, 1024], P(('grp', 'sub'))
Inputs may be any that keep to these rules, and one draw needn't show every extreme that they name: shared_count[i, j] equals shared_count[b, j xor 1] for i and its neighbour j named b; in every group some pair shares exactly 224 dofs. `shared_index`: the live slots of one subdomain toward one neighbour name distinct dofs, and every interface dof of a subdomain lies in some live slot of it. `owner`: A subdomain of group g names coarse dofs of the blocks g, g + 1, g - 1 or g + 4 (modulo 8) of 128 coarse dofs each.
All inputs are finite; a program needn't handle non-finite values.
Results may differ from a plain program's by a relative error of at most 0.012.
Values may be sent and summed in bfloat16 or wider, within the bound.
A program may use at most 192 MiB of HBM per device.

v0:
```python
import jax
import jax.numpy as jnp
from jax import lax
from jax.sharding import PartitionSpec as P


def shifted(x, axis, by):
    size = lax.axis_size(axis)
    return lax.ppermute(x, axis, [(i, (i + by) % size) for i in range(size)])


def on_device(
    iterate, load, schur, local_inverse, basis, coarse_inverse, owner, shared_index, shared_count
):
    highest = lax.Precision.HIGHEST
    width = schur.shape[1]
    columns = iterate.shape[1]
    slot_index = shared_index[0]
    slot_count = shared_count[0]
    side_total = slot_index.shape[0]
    slot_total = slot_index.shape[1]
    live = lax.broadcasted_iota(jnp.int32, (side_total, slot_total), 1) < slot_count[:, None]
    flat_index = slot_index.reshape(-1)
    live_flat = live.reshape(-1)
    multiplicity = jnp.ones((width,), jnp.float32).at[flat_index].add(live_flat.astype(jnp.float32))
    weight = (1.0 / multiplicity)[:, None]

    def outgoing(values):
        rows = jnp.take(values, flat_index, axis=0)
        rows = jnp.where(live_flat[:, None], rows, jnp.zeros_like(rows))
        return rows.reshape(side_total, slot_total, columns)

    def neighbour_rows(rows):
        pieces = []
        for reach in (1, 2, 3):
            side = 2 * (reach - 1)
            before = shifted(rows[side + 1], "sub", -reach)
            after = shifted(rows[side], "sub", reach)
            pieces.append(before)
            pieces.append(after)
        return jnp.stack(pieces)

    def add_incoming(values, incoming):
        incoming = jnp.where(live[:, :, None], incoming, jnp.zeros_like(incoming))
        return (
            values.astype(jnp.float32)
            .at[flat_index]
            .add(incoming.reshape(-1, columns).astype(jnp.float32))
        )

    product = jnp.dot(schur, iterate, preferred_element_type=jnp.float32)
    local_residual = (load.astype(jnp.float32) - product).astype(jnp.bfloat16)
    assembled = add_incoming(local_residual, neighbour_rows(outgoing(local_residual)))
    residual = assembled.astype(jnp.bfloat16)
    scaled = (weight * assembled).astype(jnp.bfloat16)
    coarse_terms = jnp.dot(basis, scaled, preferred_element_type=jnp.float32)
    coarse_total = coarse_inverse.shape[1]
    owner_ids = owner[0]
    pick = (
        lax.broadcasted_iota(jnp.int32, (owner_ids.shape[0], coarse_total), 1) == owner_ids[:, None]
    ).astype(jnp.float32)
    dense_terms = lax.dot_general(
        pick,
        coarse_terms,
        (((0,), (0,)), ((), ())),
        precision=highest,
        preferred_element_type=jnp.float32,
    )
    coarse_residual = lax.psum(dense_terms, ("grp", "sub"))
    block_values = jnp.dot(
        coarse_inverse, coarse_residual, precision=highest, preferred_element_type=jnp.float32
    )
    coarse_values = lax.all_gather(block_values, "grp", axis=0, tiled=True)
    own_values = jnp.dot(pick, coarse_values, precision=highest, preferred_element_type=jnp.float32)
    coarse_part = lax.dot_general(
        basis.astype(jnp.float32),
        own_values,
        (((0,), (0,)), ((), ())),
        precision=highest,
        preferred_element_type=jnp.float32,
    )
    local_part = jnp.dot(local_inverse, scaled, preferred_element_type=jnp.float32)
    correction = (weight * (local_part + coarse_part)).astype(jnp.bfloat16)
    update = add_incoming(correction, neighbour_rows(outgoing(correction)))
    new_iterate = (iterate.astype(jnp.float32) + update).astype(jnp.bfloat16)
    return (new_iterate, residual)


def solution(mesh):
    placed = (
        P(("grp", "sub"), None),
        P(("grp", "sub"), None),
        P(("grp", "sub"), None),
        P(("grp", "sub"), None),
        P(("grp", "sub"), None),
        P("grp", None),
        P(("grp", "sub"), None),
        P(("grp", "sub"), None, None),
        P(("grp", "sub"), None),
    )
    return jax.shard_map(
        on_device,
        mesh=mesh,
        in_specs=placed,
        out_specs=(P(("grp", "sub"), None), P(("grp", "sub"), None)),
        check_vma=False,
    )
```

profile of v0, /device:TPU:1, one launch (start us, length us, event | category | flops | bytes accessed | tf_op | source)
XLA Modules:
  0.0 529.0 jit_solution(8652872381536174075)
XLA Ops:
  9.0 7.3 %fusion.18 = (f32[1024,1024]{1,0:T(8,128)}, bf16[1024,1024]{1,0:T(8,128)(2,1)}) fusion(bf16[1024,1024]{1,0:T(8,128)(2,1)S(1)} %copy-done, bf16[1024,1024]{1,0:T(8,128)(2,1)} %param.11, bf16[1024,1024]{1,0:T(8,128)(2,1)} %param.12), kind=kOutput, calls=%fused_computation.50 | convolution fusion | flops 2151677952 | bytes 12582912 | tf_op jit(solution)/shard_map/dot_general | solution.py:51
  16.3 9.5 %gather_fusion = bf16[1344,1024]{1,0:T(8,128)(2,1)} fusion(bf16[1024,1024]{1,0:T(8,128)(2,1)} %get-tuple-element.18, s32[2048]{0:T(1024)S(1)} %pad_clamp_fusion), kind=kCustom, calls=%fused_computation.clone | custom fusion | bytes 5510400 | tf_op jit(solution)/shard_map/jit(_take)/gather | solution.py:29
  25.8 2.4 select_select_fusion.1
  29.5 8.6 %collective-permute-start = (bf16[224,1024]{1,0:T(8,128)(2,1)}, bf16[224,1024]{1,0:T(8,128)(2,1)S(1)}, u32[]{:S(2)}, u32[]{:S(2)}) collective-permute-start(bf16[224,1024]{1,0:T(8,128)(2,1)} %get-tuple-element.16), channel_id=1, source_target_pairs={{0,31},{1,0},{2,1},{3,2},{4,3},{5,4},{6,5},{7,6},{8,7},{9,8},{10,9... | collective-permute-start | bytes 1376264 | tf_op jit(solution)/shard_map/ppermute | solution.py:9
  41.0 2.4 collective-permute-start.4
  43.5 10.8 %scatter_custom_fusion = f32[1024]{0:T(1024)S(1)} fusion(s32[1344]{0:T(1024)S(1)} %fusion.11, f32[1344]{0:T(1024)S(1)} %convert_element_type.42, f32[]{:T(128)} %constant.0.clone.1), kind=kCustom, calls=%fused_computation.44 | custom fusion | flops 1344 | bytes 4100 | tf_op jit(solution)/shard_map/scatter-add | solution.py:25
  55.3 2.9 collective-permute-done.1
  58.2 15.6 %collective-permute-done.2 = bf16[224,1024]{1,0:T(8,128)(2,1)S(1)} collective-permute-done((bf16[224,1024]{1,0:T(8,128)(2,1)}, bf16[224,1024]{1,0:T(8,128)(2,1)S(1)}, u32[]{:S(2)}, u32[]{:S(2)}) %collective-permute-start.2) | collective-permute-done | bytes 458784 | tf_op jit(solution)/shard_map/ppermute | solution.py:9
  73.9 7.6 %collective-permute-done.3 = bf16[224,1024]{1,0:T(8,128)(2,1)S(1)} collective-permute-done((bf16[224,1024]{1,0:T(8,128)(2,1)}, bf16[224,1024]{1,0:T(8,128)(2,1)S(1)}, u32[]{:S(2)}, u32[]{:S(2)}) %collective-permute-start.3) | collective-permute-done | bytes 458784 | tf_op jit(solution)/shard_map/ppermute | solution.py:9
  85.6 18.0 %scatter_custom_fusion.1 = f32[1024,1024]{1,0:T(8,128)} fusion(f32[1024,1024]{1,0:T(8,128)} %get-tuple-element.17, s32[1344]{0:T(1024)S(1)} %fusion.11, bf16[1344,1024]{1,0:T(8,128)(2,1)} %bitcast_select_fusion.1), kind=kCustom, calls=%fused_computation.7 | custom fusion | flops 2752512 | bytes 6946816 | tf_op jit(solution)/shard_map/scatter-add | solution.py:48
  103.6 3.1 fusion.14
  106.8 3.9 fusion.7
  110.7 266.1 %all-reduce.2.cloned.1.call-done = f32[1024,1024]{1,0:T(8,128)} async-done(((f32[1024,1024]{1,0:T(8,128)}), f32[1024,1024]{1,0:T(8,128)}) %all-reduce.2.cloned.1.call-update) | async-done | bytes 4194320 | tf_op jit(solution)/shard_map/psum | solution.py:69
  376.8 9.6 %convolution_bitcast_fusion = f32[128,1024]{0,1:T(8,128)} fusion(f32[1024,1024]{1,0:T(8,128)} %all-reduce.2.cloned.1.call-done, f32[128,1024]{1,0:T(8,128)S(1)} %copy-done.4), kind=kOutput, calls=%fused_computation.18 | convolution fusion | flops 1610612736 | bytes 5242880 | tf_op jit(solution)/shard_map/dot_general | solution.py:70
  386.4 3.0 copy.14
  389.5 7.4 %fusion.15 = f32[1024,1024]{1,0:T(8,128)} fusion(bf16[1024,1024]{1,0:T(8,128)(2,1)} %param.14, f32[1024,1024]{1,0:T(8,128)} %scatter_custom_fusion.1, f32[1024]{0:T(1024)S(1)} %broadcast_divide_fusion), kind=kOutput, calls=%fused_computation.47 | convolution fusion | flops 2149580800 | bytes 10489856 | tf_op jit(solution)/shard_map/dot_general | solution.py:82
  396.9 28.6 %all-gather.2.cloned.1.call-done = f32[1024,1024]{0,1:T(8,128)} async-done(((f32[128,1024]{0,1:T(8,128)}), f32[1024,1024]{0,1:T(8,128)}) %all-gather.2.cloned.1.call-update) | async-done | bytes 4194320 | tf_op jit(solution)/shard_map/all_gather | solution.py:73
  425.5 4.3 fusion.5
  429.9 5.1 convert_add_fusion
  435.1 2.9 copy.15
  437.9 5.7 %gather_fusion.1 = bf16[1344,1024]{1,0:T(8,128)(2,1)} fusion(bf16[1024,1024]{1,0:T(8,128)(2,1)S(1)} %copy.15, s32[2048]{0:T(1024)S(1)} %pad_clamp_fusion), kind=kCustom, calls=%fused_computation.1.clone | custom fusion | bytes 5510400 | tf_op jit(solution)/shard_map/jit(_take)/gather | solution.py:29
  443.6 2.4 select_select_fusion
  447.3 5.2 collective-permute-start.6
  457.1 2.6 collective-permute-start.10
  459.7 5.4 %copy.16 = f32[1024,1024]{1,0:T(8,128)} copy(f32[1024,1024]{0,1:T(8,128)} %get-tuple-element.19) | data formatting | bytes 8388608 | tf_op jit(solution)/shard_map/add
  465.1 2.2 collective-permute-start.11
  467.3 5.0 collective-permute-done.7
  472.3 18.9 %collective-permute-done.8 = bf16[224,1024]{1,0:T(8,128)(2,1)S(1)} collective-permute-done((bf16[224,1024]{1,0:T(8,128)(2,1)}, bf16[224,1024]{1,0:T(8,128)(2,1)S(1)}, u32[]{:S(2)}, u32[]{:S(2)}) %collective-permute-start.8) | collective-permute-done | bytes 458784 | tf_op jit(solution)/shard_map/ppermute | solution.py:9
  491.3 2.9 collective-permute-done.9
  494.3 3.6 collective-permute-done.10
  500.0 18.1 %scatter_custom_fusion.2 = f32[1024,1024]{1,0:T(8,128)} fusion(f32[1024,1024]{1,0:T(8,128)} %copy.16, s32[1344]{0:T(1024)S(1)} %fusion.11, bf16[1344,1024]{1,0:T(8,128)(2,1)} %bitcast_select_fusion), kind=kCustom, calls=%fused_computation.5 | custom fusion | flops 2752512 | bytes 6946816 | tf_op jit(solution)/shard_map/scatter-add | solution.py:48
  518.1 3.8 convert_element_type.52
  (58 shorter events, 19.5 us)
Async XLA Ops:
  7.2 1.8 copy-start
  7.2 369.6 %all-reduce.2.cloned.1.call-start = ((), (), s32[]{:S(2)}) async-start(), calls=%async_computation | async-start | bytes 8388608 | tf_op jit(solution)/shard_map/psum | solution.py:69
  29.5 24.9 %collective-permute-start = (bf16[224,1024]{1,0:T(8,128)(2,1)}, bf16[224,1024]{1,0:T(8,128)(2,1)S(1)}, u32[]{:S(2)}, u32[]{:S(2)}) collective-permute-start(bf16[224,1024]{1,0:T(8,128)(2,1)} %get-tuple-element.16), channel_id=1, source_target_pairs={{0,31},{1,0},{2,1},{3,2},{4,3},{5,4},{6,5},{7,6},{8,7},{9,8},{10,9... | collective-permute-start | bytes 1376264 | tf_op jit(solution)/shard_map/ppermute | solution.py:9
  38.1 20.1 %collective-permute-start.1 = (bf16[224,1024]{1,0:T(8,128)(2,1)}, bf16[224,1024]{1,0:T(8,128)(2,1)S(1)}, u32[]{:S(2)}, u32[]{:S(2)}) collective-permute-start(bf16[224,1024]{1,0:T(8,128)(2,1)} %get-tuple-element.15), channel_id=1, source_target_pairs={{0,1},{1,2},{2,3},{3,4},{4,5},{5,6},{6,7},{7,8},{8,9},{9,10},{10,1... | collective-permute-start | bytes 1376264 | tf_op jit(solution)/shard_map/ppermute | solution.py:9
  38.1 35.8 %collective-permute-start.2 = (bf16[224,1024]{1,0:T(8,128)(2,1)}, bf16[224,1024]{1,0:T(8,128)(2,1)S(1)}, u32[]{:S(2)}, u32[]{:S(2)}) collective-permute-start(bf16[224,1024]{1,0:T(8,128)(2,1)} %get-tuple-element.14), channel_id=1, source_target_pairs={{0,30},{1,31},{2,0},{3,1},{4,2},{5,3},{6,4},{7,5},{8,6},{9,7},{10,... | collective-permute-start | bytes 1376264 | tf_op jit(solution)/shard_map/ppermute | solution.py:9
  39.8 41.7 %collective-permute-start.3 = (bf16[224,1024]{1,0:T(8,128)(2,1)}, bf16[224,1024]{1,0:T(8,128)(2,1)S(1)}, u32[]{:S(2)}, u32[]{:S(2)}) collective-permute-start(bf16[224,1024]{1,0:T(8,128)(2,1)} %get-tuple-element.13), channel_id=1, source_target_pairs={{0,2},{1,3},{2,4},{3,5},{4,6},{5,7},{6,8},{7,9},{8,10},{9,11},{10,... | collective-permute-start | bytes 1376264 | tf_op jit(solution)/shard_map/ppermute | solution.py:9
  41.0 42.5 %collective-permute-start.4 = (bf16[224,1024]{1,0:T(8,128)(2,1)S(1)}, bf16[224,1024]{1,0:T(8,128)(2,1)S(1)}, u32[]{:S(2)}, u32[]{:S(2)}) collective-permute-start(bf16[224,1024]{1,0:T(8,128)(2,1)S(1)} %get-tuple-element.12), channel_id=1, source_target_pairs={{0,29},{1,30},{2,31},{3,0},{4,1},{5,2},{6,3},{7,4},{8,5},{9,6},{10... | collective-permute-start | bytes 1376264 | tf_op jit(solution)/shard_map/ppermute | solution.py:9
  54.4 29.1 %collective-permute-start.5 = (bf16[224,1024]{1,0:T(8,128)(2,1)S(1)}, bf16[224,1024]{1,0:T(8,128)(2,1)S(1)}, u32[]{:S(2)}, u32[]{:S(2)}) collective-permute-start(bf16[224,1024]{1,0:T(8,128)(2,1)S(1)} %get-tuple-element.11), channel_id=1, source_target_pairs={{0,3},{1,4},{2,5},{3,6},{4,7},{5,8},{6,9},{7,10},{8,11},{9,12},{10... | collective-permute-start | bytes 1376264 | tf_op jit(solution)/shard_map/ppermute | solution.py:9
  85.6 18.0 %copy-start.5 = (bf16[24,1024]{1,0:T(8,128)(2,1)S(1)}, bf16[24,1024]{1,0:T(8,128)(2,1)}, u32[]{:S(2)}) copy-start(bf16[24,1024]{1,0:T(8,128)(2,1)} %param.15) | copy-start | bytes 147460
  103.6 3.2 copy-start.6
  110.6 266.1 %copy-start.4 = (f32[128,1024]{1,0:T(8,128)S(1)}, f32[128,1024]{1,0:T(8,128)}, u32[]{:S(2)}) copy-start(f32[128,1024]{1,0:T(8,128)} %param.16) | copy-start | bytes 1572868
  110.7 314.9 %all-gather.2.cloned.1.call-start = ((), (), s32[]{:S(2)}) async-start(), calls=%async_computation.1 | async-start | bytes 4718592 | tf_op jit(solution)/shard_map/all_gather | solution.py:73
  425.5 4.4 copy-start.3
  446.0 6.5 %copy-start.2 = (f32[1024,1024]{1,0:T(8,128)S(1)}, f32[1024,1024]{1,0:T(8,128)}, u32[]{:S(2)}) copy-start(f32[1024,1024]{1,0:T(8,128)} %scatter_custom_fusion.1) | copy-start | bytes 12582916
  447.3 17.8 %collective-permute-start.6 = (bf16[224,1024]{1,0:T(8,128)(2,1)S(1)}, bf16[224,1024]{1,0:T(8,128)(2,1)S(1)}, u32[]{:S(2)}, u32[]{:S(2)}) collective-permute-start(bf16[224,1024]{1,0:T(8,128)(2,1)S(1)} %get-tuple-element.10), channel_id=1, source_target_pairs={{0,31},{1,0},{2,1},{3,2},{4,3},{5,4},{6,5},{7,6},{8,7},{9,8},{10,9... | collective-permute-start | bytes 1376264 | tf_op jit(solution)/shard_map/ppermute | solution.py:9
  452.4 19.9 %collective-permute-start.7 = (bf16[224,1024]{1,0:T(8,128)(2,1)}, bf16[224,1024]{1,0:T(8,128)(2,1)S(1)}, u32[]{:S(2)}, u32[]{:S(2)}) collective-permute-start(bf16[224,1024]{1,0:T(8,128)(2,1)} %get-tuple-element.9), channel_id=1, source_target_pairs={{0,1},{1,2},{2,3},{3,4},{4,5},{5,6},{6,7},{7,8},{8,9},{9,10},{10,1... | collective-permute-start | bytes 1376264 | tf_op jit(solution)/shard_map/ppermute | solution.py:9
  454.1 37.2 %collective-permute-start.8 = (bf16[224,1024]{1,0:T(8,128)(2,1)}, bf16[224,1024]{1,0:T(8,128)(2,1)S(1)}, u32[]{:S(2)}, u32[]{:S(2)}) collective-permute-start(bf16[224,1024]{1,0:T(8,128)(2,1)} %get-tuple-element.8), channel_id=1, source_target_pairs={{0,30},{1,31},{2,0},{3,1},{4,2},{5,3},{6,4},{7,5},{8,6},{9,7},{10,... | collective-permute-start | bytes 1376264 | tf_op jit(solution)/shard_map/ppermute | solution.py:9
  455.9 38.3 %collective-permute-start.9 = (bf16[224,1024]{1,0:T(8,128)(2,1)}, bf16[224,1024]{1,0:T(8,128)(2,1)S(1)}, u32[]{:S(2)}, u32[]{:S(2)}) collective-permute-start(bf16[224,1024]{1,0:T(8,128)(2,1)} %get-tuple-element.7), channel_id=1, source_target_pairs={{0,2},{1,3},{2,4},{3,5},{4,6},{5,7},{6,8},{7,9},{8,10},{9,11},{10,... | collective-permute-start | bytes 1376264 | tf_op jit(solution)/shard_map/ppermute | solution.py:9
  457.1 40.8 %collective-permute-start.10 = (bf16[224,1024]{1,0:T(8,128)(2,1)}, bf16[224,1024]{1,0:T(8,128)(2,1)S(1)}, u32[]{:S(2)}, u32[]{:S(2)}) collective-permute-start(bf16[224,1024]{1,0:T(8,128)(2,1)} %get-tuple-element.6), channel_id=1, source_target_pairs={{0,29},{1,30},{2,31},{3,0},{4,1},{5,2},{6,3},{7,4},{8,5},{9,6},{10... | collective-permute-start | bytes 1376264 | tf_op jit(solution)/shard_map/ppermute | solution.py:9
  465.1 32.9 %collective-permute-start.11 = (bf16[224,1024]{1,0:T(8,128)(2,1)S(1)}, bf16[224,1024]{1,0:T(8,128)(2,1)S(1)}, u32[]{:S(2)}, u32[]{:S(2)}) collective-permute-start(bf16[224,1024]{1,0:T(8,128)(2,1)S(1)} %get-tuple-element.5), channel_id=1, source_target_pairs={{0,3},{1,4},{2,5},{3,6},{4,7},{5,8},{6,9},{7,10},{8,11},{9,12},{10... | collective-permute-start | bytes 1376264 | tf_op jit(solution)/shard_map/ppermute | solution.py:9
  500.0 22.0 %copy-start.1 = (bf16[1024,1024]{1,0:T(8,128)(2,1)S(1)}, bf16[1024,1024]{1,0:T(8,128)(2,1)}, u32[]{:S(2)}) copy-start(bf16[1024,1024]{1,0:T(8,128)(2,1)} %param.13) | copy-start | bytes 6291460
Sparse Core Ops, SparseCore 0:
  110.8 265.9 all-reduce.1
  386.6 38.9 all-gather.1
where the time goes:
time: 537 us; the launch traced here: 529 us
  waiting for transfers between devices  353 us (66%)
  other arithmetic  62.9 us (12%)
  matrix products  40.9 us (8%)
  local copies, waits for them, and re-layouts  29.7 us (6%)
  starting transfers between devices  27.8 us (5%)
  between operations  14.5 us (3%)
    psum x1, waiting for transfers between devices, on_device(): coarse_residual = lax.psum(dense_terms, ('grp', 'sub'))  266 us
    ppermute x12, waiting for transfers between devices, shifted(): return lax.ppermute(x, axis, [(i, (i + by) % size) for i in range(size)])  58.7 us
    scatter-add x2, other arithmetic, add_incoming(): return values.astype(jnp.float32).at[flat_index].add(incoming.reshape(-1,...  36.1 us
    all_gather x1, waiting for transfers between devices, on_device(): coarse_values = lax.all_gather(block_values, 'grp', axis=0, tiled=True)  28.6 us
    ppermute x12, starting transfers between devices, shifted(): return lax.ppermute(x, axis, [(i, (i + by) % size) for i in range(size)])  27.7 us
    gather x2, local copies, waits for them, and re-layouts, outgoing(): rows = jnp.take(values, flat_index, axis=0)  15.2 us
    scatter-add x1, other arithmetic, on_device(): jnp.ones((width,), jnp.float32).at[flat_index]  10.8 us
  transfers between devices with their start and end apart: 14, of which 10 were waited for; matrix products, arithmetic and copies ran while one was open for 5% of the time, Pallas kernels for 0%

commit v1 on v0

v1 whole, which is shorter than its diff:
```python
import functools

import jax
import jax.numpy as jnp
from jax import lax
from jax.experimental import pallas as pl
from jax.experimental.pallas import tpu as pltpu
from jax.sharding import PartitionSpec as P

MESH = pl.DeviceIdType.MESH
OFFSETS = (1, -1, 2, -2, 3, -3)
REL_BLOCKS = (0, 1, 4, 7)
NI = 1024
CAP = 224
SLOT = 256
SIDES = 6
NC = 24
ROWS = SIDES * SLOT
CHUNKS = 4
WIDE = NI // CHUNKS
N_SUB = 32
N_Z = 8
N_X = 4
N_GRP = 8
F32 = jnp.float32
BF16 = jnp.bfloat16


def dot(a, b):
    return jnp.dot(a, b, preferred_element_type=F32)


def dot_nt(a, b):
    return lax.dot_general(a, b, (((1,), (1,)), ((), ())), preferred_element_type=F32)


def dot_tn(a, b):
    return lax.dot_general(a, b, (((0,), (0,)), ((), ())), preferred_element_type=F32)


def split(x):
    high = x.astype(BF16)
    return high, (x - high.astype(F32)).astype(BF16)


def kernel(
    u_hbm, f_hbm, s_hbm, k_hbm, p_ref, cinv_hbm, own_ref, idx_ref,
    new_hbm, res_hbm,
    u, f, s, k, cinv, pick, pick_t, wcol, wp,
    rb, cb, out1, in1, out2, in2, stage,
    terms, gathered, etr, rel_sum, rel_in, all_sum, rel_val, own_val, near_val,
    y_out, y_in, bt,
    load_sem, a1_send, a1_recv, a2_send, a2_recv, y_send, y_recv,
    s1_send, s1_recv, s2_send, s2_recv, s3_send, s3_recv, s4_send, s4_recv,
    s5_send, s5_recv, s6_send, s6_recv, store_sem,
):
    g = lax.axis_index("grp")
    a = lax.axis_index("sub")
    z = a // N_X
    x = lax.rem(a, N_X)

    def near(j):
        return {"sub": lax.rem(a + OFFSETS[j] + N_SUB, N_SUB)}

    def along_z(d):
        return {"sub": lax.rem(z + d, N_Z) * N_X + x}

    def along_x(d):
        return {"sub": z * N_X + lax.rem(x + d, N_X)}

    def along_g(d):
        return {"grp": lax.rem(g + d, N_GRP)}

    def remote(src, dst, send, recv, where):
        return pltpu.make_async_remote_copy(
            src_ref=src, dst_ref=dst, send_sem=send, recv_sem=recv,
            device_id=where, device_id_type=MESH,
        )

    loads = [
        pltpu.make_async_copy(src, dst, load_sem.at[n])
        for n, (src, dst) in enumerate(
            ((s_hbm, s), (u_hbm, u), (f_hbm, f), (k_hbm, k), (cinv_hbm, cinv))
        )
    ]
    for load in loads:
        load.start()

    barrier = pltpu.get_barrier_semaphore()
    partners = [near(j) for j in range(SIDES)]
    partners += [along_z(d) for d in range(1, N_Z)]
    partners += [along_x(d) for d in range(1, N_X)]
    partners += [along_g(d) for d in range(1, N_GRP)]
    for who in partners:
        pl.semaphore_signal(barrier, inc=1, device_id=who, device_id_type=MESH)

    lane = lax.broadcasted_iota(jnp.int32, (SLOT, 128), 1).astype(F32)
    for j in range(SIDES):
        row = idx_ref[j : j + 1, :]
        column = jnp.transpose(jnp.broadcast_to(row, (128, SLOT)))
        for q in range(NI // 128):
            pick[SLOT * j : SLOT * (j + 1), 128 * q : 128 * (q + 1)] = jnp.where(
                column == lane + float(128 * q), 1.0, 0.0
            ).astype(BF16)

    pl.semaphore_wait(barrier, len(partners))

    def assembly_copy(out, into, send, recv, c, j):
        return remote(
            out.at[c, pl.ds(SLOT * j, CAP), :],
            into.at[c, pl.ds(SLOT * (j ^ 1), CAP), :],
            send.at[c, j],
            recv.at[c, j ^ 1],
            near(j),
        )

    def assembly_wait(out, into, send, recv, c, j):
        remote(
            out.at[c, pl.ds(SLOT * j, CAP), :],
            into.at[c, pl.ds(SLOT * j, CAP), :],
            send.at[c, j],
            recv.at[c, j],
            near(j),
        ).wait_recv()

    for n in range(3):
        loads[n].wait()

    def first(c, carry):
        columns = pl.ds(pl.multiple_of(c * WIDE, WIDE), WIDE)
        rest = (f[:, columns].astype(F32) - dot(s[...], u[:, columns])).astype(BF16)
        rb[c] = rest
        out1[c] = dot(pick[...], rest).astype(BF16)
        for j in range(SIDES):
            assembly_copy(out1, in1, a1_send, a1_recv, c, j).start()
        return carry

    lax.fori_loop(0, CHUNKS, first, 0)

    up = lax.broadcasted_iota(jnp.int32, (NI, SLOT), 0).astype(F32)
    for j in range(SIDES):
        pick_t[:, SLOT * j : SLOT * (j + 1)] = jnp.where(
            idx_ref[j : j + 1, :] == up, 1.0, 0.0
        ).astype(BF16)
    wcol[...] = 1.0 / (1.0 + dot(pick_t[...], jnp.ones((ROWS, 128), BF16)))
    wrow = 1.0 / (1.0 + dot(jnp.ones((8, ROWS), BF16), pick[...]))
    weighted = p_ref[...].astype(F32) * wrow[0:1, :]
    zero8 = jnp.zeros((8, NI), F32)
    wp[...] = jnp.concatenate([weighted, zero8], axis=0).astype(BF16)
    for j in range(SIDES):
        y_out[j] = dot_nt(wp[...], pick[SLOT * j : SLOT * (j + 1), :]).astype(BF16)
        remote(y_out.at[j], y_in.at[j ^ 1], y_send.at[j], y_recv.at[j ^ 1], near(j)).start()
    for c in range(CHUNKS):
        for j in range(SIDES):
            rows = slice(SLOT * j + CAP, SLOT * (j + 1))
            in1[c, rows, :] = jnp.zeros((SLOT - CAP, WIDE), BF16)
            in2[c, rows, :] = jnp.zeros((SLOT - CAP, WIDE), BF16)
    for n in range(N_Z):
        terms[n, NC:32, :] = own_ref[...]
        near_val[n, 7] = jnp.zeros((32, 128), BF16)
    loads[3].wait()
    loads[4].wait()

    def weights():
        return jnp.concatenate([wcol[...]] * (WIDE // 128), axis=1)

    def send_second(c):
        for j in range(SIDES):
            assembly_copy(out2, in2, a2_send, a2_recv, c, j).start()

    def second(c, carry):
        for j in range(SIDES):
            assembly_wait(out1, in1, a1_send, a1_recv, c, j)
        total = rb[c].astype(F32) + dot(pick_t[...], in1[c])
        columns = pl.ds(pl.multiple_of(c * WIDE, WIDE), WIDE)
        stage[0, c] = total.astype(BF16)
        pltpu.make_async_copy(stage.at[0, c], res_hbm.at[:, columns], store_sem.at[0, c]).start()
        scaled = (weights() * total).astype(BF16)
        part = dot(p_ref[...], scaled)
        for q in range(WIDE // 128):
            terms[c * (WIDE // 128) + q, 0:NC, :] = part[:, 128 * q : 128 * (q + 1)]
        local = (weights() * dot(k[...], scaled)).astype(BF16)
        cb[c] = local
        out2[c] = dot(pick[...], local).astype(BF16)

        @pl.when(c == 0)
        def _():
            send_second(c)

        return carry

    lax.fori_loop(0, CHUNKS, second, 0)

    def z_copy(d):
        there = lax.rem(z + d, N_Z)
        return remote(
            terms.at[there], gathered.at[x, z], s1_send.at[d - 1], s1_recv.at[d - 1], along_z(d)
        )

    for d in range(1, N_Z):
        z_copy(d).start()
    gathered[x, z] = terms[z]
    for d in range(1, N_Z):
        here = lax.rem(z + N_Z - d, N_Z)
        remote(
            terms.at[z], gathered.at[x, here], s1_send.at[d - 1], s1_recv.at[d - 1], along_z(d)
        ).wait_recv()

    def x_copy(d):
        return remote(
            gathered.at[x], gathered.at[x], s2_send.at[d - 1], s2_recv.at[d - 1], along_x(d)
        )

    for d in range(1, N_X):
        x_copy(d).start()

    def issue(c, carry):
        send_second(c)
        return carry

    lax.fori_loop(1, CHUNKS, issue, 0)

    for j in range(SIDES):
        remote(y_out.at[j], y_in.at[j], y_send.at[j], y_recv.at[j], near(j)).wait_recv()
    blocks = []
    for t in range(7):
        o = t - 3
        if o == 0:
            blocks.append(wp[...].astype(F32))
        else:
            j = OFFSETS.index(o)
            blocks.append(dot(y_in[j], pick[SLOT * j : SLOT * (j + 1), :]))
    blocks.append(jnp.zeros((32, NI), F32))
    bt[...] = jnp.transpose(jnp.concatenate(blocks, axis=0)).astype(BF16)

    for d in range(1, N_X):
        here = lax.rem(x + N_X - d, N_X)
        remote(
            gathered.at[x], gathered.at[here], s2_send.at[d - 1], s2_recv.at[d - 1], along_x(d)
        ).wait_recv()

    column512 = lax.broadcasted_iota(jnp.int32, (32, 512), 1)
    block = column512 // 128
    names = (
        column512 - block * 128
        + jnp.where(block == 1, 128, jnp.where(block == 2, 512, jnp.where(block == 3, 896, 0)))
    ).astype(F32)
    base = (g * 128).astype(F32)
    for xx in range(N_X):
        plane = jnp.concatenate([gathered[xx, zz] for zz in range(N_Z)], axis=0)
        turned = jnp.transpose(plane)
        for zz in range(N_Z):
            who = turned[0:32, 32 * zz + NC : 32 * zz + NC + 1]
            rel = who - base
            rel = jnp.where(rel < 0.0, rel + 1024.0, rel)
            rel = jnp.where(who < 0.0, -1.0, rel)
            etr[256 * xx + 32 * zz : 256 * xx + 32 * (zz + 1), :] = jnp.where(
                rel == names, 1.0, 0.0
            ).astype(BF16)
    flat = jnp.concatenate(
        [gathered[xx, zz] for xx in range(N_X) for zz in range(N_Z)], axis=0
    )
    high, low = split(flat)
    sums = dot_tn(etr[...], high) + dot_tn(etr[...], low)
    for n in range(4):
        rel_sum[n] = sums[128 * n : 128 * (n + 1), :]
    for n in range(1, 4):
        remote(
            rel_sum.at[n], rel_in.at[n - 1], s3_send.at[n - 1], s3_recv.at[n - 1],
            along_g(REL_BLOCKS[n]),
        ).start()
    for n in range(1, 4):
        remote(
            rel_sum.at[n], rel_in.at[n - 1], s3_send.at[n - 1], s3_recv.at[n - 1],
            along_g(REL_BLOCKS[n]),
        ).wait_recv()
    all_sum[g] = rel_sum[0] + rel_in[0] + rel_in[1] + rel_in[2]
    for d in range(1, N_GRP):
        remote(
            all_sum.at[g], all_sum.at[g], s4_send.at[d - 1], s4_recv.at[d - 1], along_g(d)
        ).start()
    for d in range(1, N_GRP):
        here = lax.rem(g + N_GRP - d, N_GRP)
        remote(
            all_sum.at[g], all_sum.at[here], s4_send.at[d - 1], s4_recv.at[d - 1], along_g(d)
        ).wait_recv()
    high, low = split(all_sum[...].reshape(NI, 128))
    chigh, clow = split(cinv[...])
    rel_val[0] = dot(chigh, high) + (dot(chigh, low) + dot(clow, high))
    for n, d in ((1, 7), (2, 4), (3, 1)):
        remote(
            rel_val.at[0], rel_val.at[n], s5_send.at[n - 1], s5_recv.at[n - 1], along_g(d)
        ).start()
    for n, d in ((1, 7), (2, 4), (3, 1)):
        remote(
            rel_val.at[0], rel_val.at[n], s5_send.at[n - 1], s5_recv.at[n - 1], along_g(d)
        ).wait_recv()
    high, low = split(rel_val[...].reshape(512, 128))
    values = (dot(etr[...], high) + dot(etr[...], low)).astype(BF16)
    for xx in range(N_X):
        for zz in range(N_Z):
            piece = values[256 * xx + 32 * zz : 256 * xx + 32 * (zz + 1), :]
            place = zz * N_X + xx + 3
            own_val[place] = piece
            if place >= N_SUB:
                own_val[place - N_SUB] = piece
            if place < 6:
                own_val[place + N_SUB] = piece
    for d in range(1, N_Z):
        there = lax.rem(z + d, N_Z)
        remote(
            own_val.at[pl.ds(there * N_X + x, 7)], near_val.at[z, pl.ds(0, 7)],
            s6_send.at[d - 1], s6_recv.at[d - 1], along_z(d),
        ).start()
    near_val[z, pl.ds(0, 7)] = own_val[pl.ds(a, 7)]
    for d in range(1, N_Z):
        here = lax.rem(z + N_Z - d, N_Z)
        remote(
            own_val.at[pl.ds(a, 7)], near_val.at[here, pl.ds(0, 7)],
            s6_send.at[d - 1], s6_recv.at[d - 1], along_z(d),
        ).wait_recv()

    def third(c, carry):
        columns = pl.ds(pl.multiple_of(c * WIDE, WIDE), WIDE)
        coarse = jnp.concatenate(
            [near_val[c * (WIDE // 128) + q].reshape(256, 128) for q in range(WIDE // 128)], axis=1
        )
        part = u[:, columns].astype(F32) + (cb[c].astype(F32) + dot(bt[...], coarse))
        for j in range(SIDES):
            assembly_wait(out2, in2, a2_send, a2_recv, c, j)
        stage[1, c] = (part + dot(pick_t[...], in2[c])).astype(BF16)
        pltpu.make_async_copy(stage.at[1, c], new_hbm.at[:, columns], store_sem.at[1, c]).start()
        return carry

    lax.fori_loop(0, CHUNKS, third, 0)

    def finish(c, carry):
        columns = pl.ds(pl.multiple_of(c * WIDE, WIDE), WIDE)
        for j in range(SIDES):
            assembly_copy(out1, in1, a1_send, a1_recv, c, j).wait_send()
            assembly_copy(out2, in2, a2_send, a2_recv, c, j).wait_send()
        pltpu.make_async_copy(stage.at[0, c], res_hbm.at[:, columns], store_sem.at[0, c]).wait()
        pltpu.make_async_copy(stage.at[1, c], new_hbm.at[:, columns], store_sem.at[1, c]).wait()
        return carry

    lax.fori_loop(0, CHUNKS, finish, 0)
    for j in range(SIDES):
        remote(y_out.at[j], y_in.at[j ^ 1], y_send.at[j], y_recv.at[j ^ 1], near(j)).wait_send()
    for d in range(1, N_Z):
        z_copy(d).wait_send()
        there = lax.rem(z + d, N_Z)
        remote(
            own_val.at[pl.ds(there * N_X + x, 7)], near_val.at[z, pl.ds(0, 7)],
            s6_send.at[d - 1], s6_recv.at[d - 1], along_z(d),
        ).wait_send()
        remote(
            all_sum.at[g], all_sum.at[g], s4_send.at[d - 1], s4_recv.at[d - 1], along_g(d)
        ).wait_send()
    for d in range(1, N_X):
        x_copy(d).wait_send()
    for n in range(1, 4):
        remote(
            rel_sum.at[n], rel_in.at[n - 1], s3_send.at[n - 1], s3_recv.at[n - 1],
            along_g(REL_BLOCKS[n]),
        ).wait_send()
        remote(
            rel_val.at[0], rel_val.at[n], s5_send.at[n - 1], s5_recv.at[n - 1], along_g(1)
        ).wait_send()


def on_device(
    iterate, load, schur, local_inverse, basis, coarse_inverse, owner, shared_index, shared_count
):
    live = lax.broadcasted_iota(jnp.int32, (SIDES, CAP), 1) < shared_count[0][:, None]
    index = jnp.where(live, shared_index[0], -1).astype(F32)
    index = jnp.pad(index, ((0, 8 - SIDES), (0, SLOT - CAP)), constant_values=-1.0)
    names = jnp.pad(owner.astype(F32), ((0, 0), (0, 128 - NC)), constant_values=-1.0)
    names = jnp.broadcast_to(names, (8, 128))
    anywhere = pl.BlockSpec(memory_space=pl.ANY)
    vmem = pl.BlockSpec(memory_space=pltpu.VMEM)
    square = jax.ShapeDtypeStruct((NI, NI), BF16)
    dma = pltpu.SemaphoreType.DMA
    new, residual = pl.pallas_call(
        kernel,
        out_shape=(square, square),
        in_specs=[anywhere, anywhere, anywhere, anywhere, vmem, anywhere, vmem, vmem],
        out_specs=(anywhere, anywhere),
        scratch_shapes=[
            pltpu.VMEM((NI, NI), BF16),
            pltpu.VMEM((NI, NI), BF16),
            pltpu.VMEM((NI, NI), BF16),
            pltpu.VMEM((NI, NI), BF16),
            pltpu.VMEM((128, NI), F32),
            pltpu.VMEM((ROWS, NI), BF16),
            pltpu.VMEM((NI, ROWS), BF16),
            pltpu.VMEM((NI, 128), F32),
            pltpu.VMEM((32, NI), BF16),
            pltpu.VMEM((CHUNKS, NI, WIDE), BF16),
            pltpu.VMEM((CHUNKS, NI, WIDE), BF16),
            pltpu.VMEM((CHUNKS, ROWS, WIDE), BF16),
            pltpu.VMEM((CHUNKS, ROWS, WIDE), BF16),
            pltpu.VMEM((CHUNKS, ROWS, WIDE), BF16),
            pltpu.VMEM((CHUNKS, ROWS, WIDE), BF16),
            pltpu.VMEM((2, CHUNKS, NI, WIDE), BF16),
            pltpu.VMEM((N_Z, 32, 128), F32),
            pltpu.VMEM((N_X, N_Z, 32, 128), F32),
            pltpu.VMEM((NI, 512), BF16),
            pltpu.VMEM((4, 128, 128), F32),
            pltpu.VMEM((3, 128, 128), F32),
            pltpu.VMEM((N_GRP, 128, 128), F32),
            pltpu.VMEM((4, 128, 128), F32),
            pltpu.VMEM((N_SUB + 6, 32, 128), BF16),
            pltpu.VMEM((N_Z, 8, 32, 128), BF16),
            pltpu.VMEM((SIDES, 32, SLOT), BF16),
            pltpu.VMEM((SIDES, 32, SLOT), BF16),
            pltpu.VMEM((NI, 256), BF16),
            dma((5,)),
            dma((CHUNKS, SIDES)),
            dma((CHUNKS, SIDES)),
            dma((CHUNKS, SIDES)),
            dma((CHUNKS, SIDES)),
            dma((SIDES,)),
            dma((SIDES,)),
            dma((7,)), dma((7,)),
            dma((3,)), dma((3,)),
            dma((3,)), dma((3,)),
            dma((7,)), dma((7,)),
            dma((3,)), dma((3,)),
            dma((7,)), dma((7,)),
            dma((2, CHUNKS)),
        ],
        compiler_params=pltpu.CompilerParams(
            collective_id=0, has_side_effects=True, vmem_limit_bytes=60 * 1024 * 1024
        ),
        name="bddc_step",
    )(iterate, load, schur, local_inverse, basis, coarse_inverse, names, index)
    return new, residual


def solution(mesh):
    rows = P(("grp", "sub"), None)
    placed = (rows, rows, rows, rows, rows, P("grp", None), rows, P(("grp", "sub"), None, None), rows)
    return jax.shard_map(
        on_device, mesh=mesh, in_specs=placed, out_specs=(rows, rows), check_vma=False
    )
```

time: 537 us -> 144 us (0.27); the launches traced: 529 us -> 144 us
  waiting for transfers between devices: 353 us -> 0 us
  Pallas kernels: 0 us -> 136 us
  other arithmetic: 62.9 us -> 1.42 us
  matrix products: 40.9 us -> 0 us
  starting transfers between devices: 27.8 us -> 0 us
  local copies, waits for them, and re-layouts: 29.7 us -> 5.76 us
  between operations: 14.5 us -> 0.65 us
    psum x1 -> x0, waiting for transfers between devices: 266 us -> none  [on_device(): coarse_residual = lax.psum(dense_terms, ('grp', 'sub'))]
    pallas_call x0 -> x1, Pallas kernels: none -> 136 us  [on_device(): pl.pallas_call(kernel, out_shape=(square, square), in_specs=[anywhere, an...]
    ppermute x12 -> x0, waiting for transfers between devices: 58.7 us -> none  [shifted(): return lax.ppermute(x, axis, [(i, (i + by) % size) for i in range(size)])]
    scatter-add x3 -> x0, other arithmetic: 47 us -> none  [the longest x2 36.1 us: add_incoming(): return values.astype(jnp.float32).at[flat_index].add(incoming.reshape(-1,...]
    dot_general x7 -> x0, matrix products: 40.9 us -> none  [the longest x1 9.64 us: on_device(): jnp.dot(coarse_inverse, coarse_residual, precision=highest, preferred_ele...]
    all_gather x1 -> x0, waiting for transfers between devices: 28.6 us -> none  [on_device(): coarse_values = lax.all_gather(block_values, 'grp', axis=0, tiled=True)]
    ppermute x12 -> x0, starting transfers between devices: 27.7 us -> none  [shifted(): return lax.ppermute(x, axis, [(i, (i + by) % size) for i in range(size)])]
    gather x2 -> x0, local copies, waits for them, and re-layouts: 15.2 us -> none  [outgoing(): rows = jnp.take(values, flat_index, axis=0)]
  transfers between devices with their start and end apart: 14 -> 0, of which waited for: 10 -> 0; matrix products, arithmetic and copies ran while one was open for 5% -> 0% of each run, Pallas kernels for 0% -> 0%
where the time goes in v1:
time: 144 us
  Pallas kernels  136 us (94%)
  local copies, waits for them, and re-layouts  5.76 us (4%)
    pallas_call x1, Pallas kernels, on_device(): pl.pallas_call(kernel, out_shape=(square, square), in_specs=[anywhere, an...  136 us
    unnamed x4, local copies, waits for them, and re-layouts  4.55 us

profile of v1, /device:TPU:1, one launch (start us, length us, event | category | flops | bytes accessed | tf_op | source)
XLA Modules:
  0.0 143.5 jit_solution(15121836120819934461)
XLA Ops:
  0.6 0.7 convert_element_type.6
  1.3 0.6 broadcast_in_dim.12.own_ref
  1.9 0.8 fusion
  2.7 0.6 pad.9.idx_ref
  3.3 135.7 %bddc_step.1 = (bf16[1024,1024]{1,0:T(8,128)(2,1)}, bf16[1024,1024]{1,0:T(8,128)(2,1)}) custom-call(bf16[1024,1024]{1,0:T(8,128)(2,1)} %u_hbm.1, bf16[1024,1024]{1,0:T(8,128)(2,1)} %f_hbm.1, bf16[1024,1024]{1,0:T(8,128)(2,1)} %s_hbm.1, bf16[1024,1024]{1,0:T(8,128)(2,1)} %k_hbm.1, bf16[24,1024]{1,0:T(8,128)(2,1)} %p_ref.1, f32[128,1024]{1,0:T(8,128)} %cinv_hbm.1, ...), custom_call_target="tpu_custom_call" | custom-call | tf_op jit(solution)/shard_map/bddc_step/pallas_call | solution.py:383
  139.0 0.0 copy-start
  139.0 3.2 %copy.15 = bf16[1024,1024]{1,0:T(8,128)(2,1)} copy(bf16[1024,1024]{1,0:T(8,128)(2,1)} %get-tuple-element.4) | data formatting | bytes 4194304
  142.2 0.0 copy-done
  142.2 1.3 copy.16
  (1 shorter events, 0.0 us)
Async XLA Ops:
  139.0 3.2 %copy-start = (bf16[1024,1024]{1,0:T(8,128)(2,1)S(1)}, bf16[1024,1024]{1,0:T(8,128)(2,1)}, u32[]{:S(2)}) copy-start(bf16[1024,1024]{1,0:T(8,128)(2,1)} %get-tuple-element.5) | copy-start | bytes 6291460

commit v2 on v0

v2 whole, which is shorter than its diff:
```python
import jax
import jax.numpy as jnp
from jax import lax
from jax.experimental import pallas as pl
from jax.experimental.pallas import tpu as pltpu
from jax.sharding import PartitionSpec as P

MESH = pl.DeviceIdType.MESH
OFFSETS = (1, -1, 2, -2, 3, -3)
NI = 1024
CAP = 224
SLOT = 256
SIDES = 6
NC = 24
ROWS = SIDES * SLOT
CHUNKS = 4
WIDE = NI // CHUNKS
N_SUB = 32
N_Z = 8
N_X = 4
N_GRP = 8
NCG = 1024
LIMIT = 49 * 1024 * 1024
EARLY = 2
PER = WIDE // 128
TALL = 176
F32 = jnp.float32
BF16 = jnp.bfloat16


def dot(a, b):
    return jnp.dot(a, b, preferred_element_type=F32)


def dot_nt(a, b):
    return lax.dot_general(a, b, (((1,), (1,)), ((), ())), preferred_element_type=F32)


def dot_tn(a, b):
    return lax.dot_general(a, b, (((0,), (0,)), ((), ())), preferred_element_type=F32)


def split(x):
    high = x.astype(BF16)
    return high, (x - high.astype(F32)).astype(BF16)


def kernel(
    u_hbm, f_hbm, s_hbm, k_hbm, p_ref, cinv_hbm, own_ref, idx_ref, cnt_ref,
    new_ref, res_ref,
    u, f, s, k, cinv, slots, pick, pick_t, wcol, wp,
    rb, cb, out1, in1, out2, in2,
    owners, btr, bt, y_out, y_in, terms, terms_in, etr, t_out, t_in, pieces,
    v_out, v_in, rel_val, own_val, near_val, early,
    load_sem, a1_send, a1_recv, a2_send, a2_recv, y_send, y_recv,
    s1_send, s1_recv, s2_send, s2_recv, s3_send, s3_recv, s4_send, s4_recv,
    s5_send, s5_recv, s6_send, s6_recv,
):
    g = lax.axis_index("grp")
    a = lax.axis_index("sub")
    z = a // N_X
    x = lax.rem(a, N_X)

    def near(j):
        return {"sub": lax.rem(a + OFFSETS[j] + N_SUB, N_SUB)}

    def along_z(d):
        return {"sub": lax.rem(z + d, N_Z) * N_X + x}

    def along_x(d):
        return {"sub": z * N_X + lax.rem(x + d, N_X)}

    def along_g(d):
        return {"grp": lax.rem(g + d, N_GRP)}

    def remote(src, dst, send, recv, where):
        return pltpu.make_async_remote_copy(
            src_ref=src, dst_ref=dst, send_sem=send, recv_sem=recv,
            device_id=where, device_id_type=MESH,
        )

    loads = [pltpu.make_async_copy(s_hbm, s, load_sem.at[0])]
    for c in range(CHUNKS):
        cols = pl.ds(c * WIDE, WIDE)
        for n, (src, dst) in enumerate(((u_hbm, u), (f_hbm, f))):
            loads.append(
                pltpu.make_async_copy(src.at[:, cols], dst.at[c], load_sem.at[1 + 2 * c + n])
            )
    late_loads = [
        pltpu.make_async_copy(k_hbm, k, load_sem.at[1 + 2 * CHUNKS]),
        pltpu.make_async_copy(cinv_hbm, cinv, load_sem.at[2 + 2 * CHUNKS]),
    ]
    for load in loads + late_loads:
        load.start()

    barrier = pltpu.get_barrier_semaphore()
    partners = [near(j) for j in range(SIDES)]
    partners += [along_z(d) for d in range(1, N_Z)]
    partners += [along_x(d) for d in range(1, N_X)]
    partners += [along_g(d) for d in range(1, N_GRP)]
    for who in partners:
        pl.semaphore_signal(barrier, inc=1, device_id=who, device_id_type=MESH)

    slots[...] = jnp.full((8, SLOT), -1.0, F32)
    slot_ids = lax.broadcasted_iota(jnp.int32, (1, CAP), 1)
    for j in range(SIDES):
        slots[j : j + 1, 0:CAP] = jnp.where(
            slot_ids < cnt_ref[0, j], idx_ref[0, j : j + 1, :].astype(F32), -1.0
        )
    lane = lax.broadcasted_iota(jnp.int32, (SLOT, 128), 1).astype(F32)
    counts = [jnp.zeros((8, 128), F32)] * (NI // 128)
    for j in range(SIDES):
        column = jnp.transpose(jnp.broadcast_to(slots[j : j + 1, :], (128, SLOT)))
        for q in range(NI // 128):
            hot = jnp.where(column == lane + float(128 * q), 1.0, 0.0)
            pick[SLOT * j : SLOT * (j + 1), 128 * q : 128 * (q + 1)] = hot.astype(BF16)
            counts[q] += jnp.sum(hot.reshape(SLOT // 8, 8, 128), axis=0)
    wrow = 1.0 / (1.0 + jnp.sum(jnp.concatenate(counts, axis=1), axis=0, keepdims=True))

    def first(c):
        if c == 0:
            loads[0].wait()
        loads[1 + 2 * c].wait()
        loads[2 + 2 * c].wait()
        rest = (f[c].astype(F32) - dot(s[...], u[c])).astype(BF16)
        rb[c] = rest
        out1[c] = dot(pick[...], rest).astype(BF16)

    def assembly_copy(out, into, send, recv, c, j):
        return remote(
            out.at[c, pl.ds(SLOT * j, CAP), :],
            into.at[c, pl.ds(SLOT * (j ^ 1), CAP), :],
            send.at[c, j],
            recv.at[c, j ^ 1],
            near(j),
        )

    def assembly_wait(out, into, send, recv, c, j):
        remote(
            out.at[c, pl.ds(SLOT * j, CAP), :],
            into.at[c, pl.ds(SLOT * j, CAP), :],
            send.at[c, j],
            recv.at[c, j],
            near(j),
        ).wait_recv()

    def send_first(c):
        for j in range(SIDES):
            assembly_copy(out1, in1, a1_send, a1_recv, c, j).start()

    def send_second(c, sides=range(SIDES)):
        for j in sides:
            assembly_copy(out2, in2, a2_send, a2_recv, c, j).start()

    weighted = p_ref[...].astype(F32) * wrow
    wp[...] = jnp.concatenate([weighted, jnp.zeros((8, NI), F32)], axis=0).astype(BF16)
    owners[...] = jnp.zeros((16, 128), F32)
    owners[8:9, 0:NC] = (own_ref[...] >> 5).astype(F32)
    owners[9:10, 0:NC] = (own_ref[...] & 31).astype(F32)
    low_names = pltpu.roll(jnp.broadcast_to(owners[9:10, :], (8, 128)), 64, 1)
    mine = jnp.broadcast_to(owners[8:9, :], (8, 128)) + low_names
    for j in range(SIDES):
        rows = dot_nt(wp[...], pick[SLOT * j : SLOT * (j + 1), :])
        tail = jnp.concatenate([mine, jnp.zeros((8, SLOT - 128), F32)], axis=1)
        y_out[j] = jnp.concatenate([rows[0:NC], tail], axis=0).astype(BF16)
    first(0)
    pl.semaphore_wait(barrier, len(partners))
    for j in range(SIDES):
        remote(y_out.at[j], y_in.at[j ^ 1], y_send.at[j], y_recv.at[j ^ 1], near(j)).start()
    send_first(0)

    for c in range(1, CHUNKS):
        first(c)
        if c < 2:
            send_first(c)

    for j in range(SIDES):
        remote(y_out.at[j], y_in.at[j], y_send.at[j], y_recv.at[j], near(j)).wait_recv()
    blocks = []
    for t in range(7):
        if t == 3:
            blocks.append(wp[0:NC, :].astype(F32))
            owners[t : t + 1, :] = mine[0:1, :]
        else:
            j = OFFSETS.index(t - 3)
            blocks.append(dot(y_in[j], pick[SLOT * j : SLOT * (j + 1), :])[0:NC])
            owners[t : t + 1, :] = y_in[j, NC:32, 0:128].astype(F32)[0:1, :]
    blocks.append(jnp.zeros((256 - 7 * NC, NI), F32))
    every = jnp.concatenate(blocks, axis=0)
    btr[...] = every[0:TALL].astype(BF16)
    for c in range(CHUNKS):
        part = dot(btr[...], rb[c])
        for q in range(PER):
            terms[c * PER + q] = jnp.concatenate(
                [part[0 : 7 * NC, 128 * q : 128 * (q + 1)], owners[0:8, :]], axis=0
            ).astype(BF16)

    def z_copy(d):
        there = lax.rem(z + d, N_Z)
        return remote(
            terms.at[there], terms_in.at[z], s1_send.at[d - 1], s1_recv.at[d - 1], along_z(d)
        )

    for d in range(1, N_Z):
        z_copy(d).start()
    send_first(2)
    terms_in[z] = terms[z]

    up = lax.broadcasted_iota(jnp.int32, (NI, SLOT), 0).astype(F32)
    for j in range(SIDES):
        pick_t[:, SLOT * j : SLOT * (j + 1)] = jnp.where(
            slots[j : j + 1, :] == up, 1.0, 0.0
        ).astype(BF16)
    wcol[...] = 1.0 / (1.0 + dot(pick_t[...], jnp.ones((ROWS, 128), BF16)))
    for c in range(CHUNKS):
        for j in range(SIDES):
            rows = slice(SLOT * j + CAP, SLOT * (j + 1))
            in1[c, rows, :] = jnp.zeros((SLOT - CAP, WIDE), BF16)
            in2[c, rows, :] = jnp.zeros((SLOT - CAP, WIDE), BF16)
    for n in range(N_Z):
        near_val[n, TALL:256, :] = jnp.zeros((256 - TALL, 128), BF16)
    for load in late_loads:
        load.wait()

    bt[...] = jnp.transpose(every).astype(BF16)
    for d in range(1, N_Z):
        here = lax.rem(z + N_Z - d, N_Z)
        remote(
            terms.at[z], terms_in.at[here], s1_send.at[d - 1], s1_recv.at[d - 1], along_z(d)
        ).wait_recv()

    weights = jnp.concatenate([wcol[...]] * (WIDE // 128), axis=1)

    def second(c):
        for j in range(SIDES):
            assembly_wait(out1, in1, a1_send, a1_recv, c, j)
        total = rb[c].astype(F32) + dot(pick_t[...], in1[c])
        res_ref[:, c * WIDE : (c + 1) * WIDE] = total.astype(BF16)
        scaled = (weights * total).astype(BF16)
        local = (weights * dot(k[...], scaled)).astype(BF16)
        cb[c] = local
        out2[c] = dot(pick[...], local).astype(BF16)

    column512 = lax.broadcasted_iota(jnp.int32, (NC, 512), 1)
    block = column512 // 128
    start = block + 2 * (block // 2) + 2 * (block // 3)
    names = (column512 + 128 * (start - block)).astype(F32)
    base = (g * 128).astype(F32)
    turned = jnp.transpose(
        jnp.concatenate([terms_in[n, TALL - 16 : TALL, :].astype(F32)[8:16] for n in range(N_Z)], axis=0)
    )
    who = turned[0:NC, :] * 32.0 + turned[64 : 64 + NC, :]
    rel = who - base
    rel = jnp.where(rel < 0.0, rel + float(NCG), rel)
    for n in range(N_Z):
        hot = [
            jnp.where(rel[:, 8 * n + t : 8 * n + t + 1] == names, 1.0, 0.0) for t in range(7)
        ]
        hot.append(jnp.zeros((8, 512), F32))
        etr[TALL * n : TALL * (n + 1), :] = jnp.concatenate(hot, axis=0).astype(BF16)
    sums = dot_tn(etr[...], terms_in[...].reshape(N_Z * TALL, 128)).reshape(4, 128, 128)
    t_out[...] = sums.astype(BF16)

    def x_copy(d):
        there = lax.rem(x + d, N_X)
        return remote(
            t_out.at[there], t_in.at[d - 1], s2_send.at[d - 1], s2_recv.at[d - 1], along_x(d)
        )

    for d in range(1, N_X):
        x_copy(d).start()
    second(0)
    send_first(3)
    for d in range(1, N_X):
        x_copy(d).wait_recv()
    own_block = t_out[x].astype(F32)
    for d in range(1, N_X):
        own_block += t_in[d - 1].astype(F32)
    named = lax.rem(g + x + 2 * (x // 2) + 2 * (x // 3), N_GRP)
    pieces[named] = own_block.astype(BF16)

    def g_copy(d):
        return remote(
            pieces.at[named], pieces.at[named], s3_send.at[d - 1], s3_recv.at[d - 1], along_g(d)
        )

    for d in range(1, N_GRP):
        g_copy(d).start()
    send_second(0)
    second(1)
    for d in range(1, N_GRP):
        here = lax.rem(named + N_GRP - d, N_GRP)
        remote(
            pieces.at[named], pieces.at[here], s3_send.at[d - 1], s3_recv.at[d - 1], along_g(d)
        ).wait_recv()
    chigh, clow = split(cinv[...])
    flat = pieces[...].reshape(NI, 128)
    partial = dot(chigh, flat) + dot(clow, flat)
    v_out[0] = partial.astype(BF16)

    def v_copy(d):
        return remote(
            v_out.at[0], v_in.at[d - 1], s4_send.at[d - 1], s4_recv.at[d - 1], along_x(d)
        )

    for d in range(1, N_X):
        v_copy(d).start()
    send_second(1, range(3))
    second(2)
    send_second(1, range(3, SIDES))
    for d in range(1, N_X):
        v_copy(d).wait_recv()
    solved = v_out[0].astype(F32)
    for d in range(1, N_X):
        solved += v_in[d - 1].astype(F32)
    rel_val[0] = solved.astype(BF16)

    def r_copy(n):
        return remote(
            rel_val.at[0], rel_val.at[n], s5_send.at[n - 1], s5_recv.at[n - 1],
            along_g((7, 4, 1)[n - 1]),
        )

    for n in range(1, 4):
        r_copy(n).start()
    send_second(2)
    second(3)
    for n in range(1, 4):
        r_copy(n).wait_recv()
    own_val[...] = dot(etr[...], rel_val[...].reshape(512, 128)).astype(BF16).reshape(N_Z, TALL, 128)

    def o_copy(d):
        there = lax.rem(z + d, N_Z)
        return remote(
            own_val.at[there], near_val.at[z, pl.ds(0, TALL)],
            s6_send.at[d - 1], s6_recv.at[d - 1], along_z(d),
        )

    for d in range(1, N_Z):
        o_copy(d).start()
    send_second(3)
    near_val[z, pl.ds(0, TALL)] = own_val[z]

    def second_sum(c):
        for j in range(SIDES):
            assembly_wait(out2, in2, a2_send, a2_recv, c, j)
        return u[c].astype(F32) + (cb[c].astype(F32) + dot(pick_t[...], in2[c]))

    for c in range(EARLY):
        early[c] = second_sum(c)
    for d in range(1, N_Z):
        here = lax.rem(z + N_Z - d, N_Z)
        remote(
            own_val.at[z], near_val.at[here, pl.ds(0, TALL)],
            s6_send.at[d - 1], s6_recv.at[d - 1], along_z(d),
        ).wait_recv()

    def third(c):
        coarse = dot(bt[...], jnp.concatenate([near_val[c * PER + q] for q in range(PER)], axis=1))
        if c < EARLY:
            total = early[c] + coarse
        else:
            total = u[c].astype(F32) + (cb[c].astype(F32) + coarse)
            for j in range(SIDES):
                assembly_wait(out2, in2, a2_send, a2_recv, c, j)
            total += dot(pick_t[...], in2[c])
        new_ref[:, c * WIDE : (c + 1) * WIDE] = total.astype(BF16)

    for c in range(CHUNKS):
        third(c)

    for c in range(CHUNKS):
        for j in range(SIDES):
            assembly_copy(out1, in1, a1_send, a1_recv, c, j).wait_send()
            assembly_copy(out2, in2, a2_send, a2_recv, c, j).wait_send()
    for j in range(SIDES):
        remote(y_out.at[j], y_in.at[j ^ 1], y_send.at[j], y_recv.at[j ^ 1], near(j)).wait_send()
    for d in range(1, N_Z):
        z_copy(d).wait_send()
        o_copy(d).wait_send()
        g_copy(d).wait_send()
    for d in range(1, N_X):
        x_copy(d).wait_send()
        v_copy(d).wait_send()
    for n in range(1, 4):
        r_copy(n).wait_send()


def on_device(
    iterate, load, schur, local_inverse, basis, coarse_inverse, owner, shared_index, shared_count
):
    anywhere = pl.BlockSpec(memory_space=pltpu.HBM)
    vmem = pl.BlockSpec(memory_space=pltpu.VMEM)
    smem = pl.BlockSpec(memory_space=pltpu.SMEM)
    square = jax.ShapeDtypeStruct((NI, NI), BF16)
    dma = pltpu.SemaphoreType.DMA

    def bf16(*shape):
        return pltpu.VMEM(shape, BF16)

    def f32(*shape):
        return pltpu.VMEM(shape, F32)

    chunk = (CHUNKS, NI, WIDE)
    side = (CHUNKS, ROWS, WIDE)
    return pl.pallas_call(
        kernel,
        out_shape=(square, square),
        in_specs=[anywhere, anywhere, anywhere, anywhere, vmem, anywhere, vmem, vmem, smem],
        out_specs=(vmem, vmem),
        scratch_shapes=[
            bf16(*chunk), bf16(*chunk), bf16(NI, NI), bf16(NI, NI), f32(128, NI),
            f32(8, SLOT), bf16(ROWS, NI), bf16(NI, ROWS), f32(NI, 128), bf16(32, NI),
            bf16(*chunk), bf16(*chunk), bf16(*side), bf16(*side), bf16(*side), bf16(*side),
            f32(16, 128), bf16(TALL, NI), bf16(NI, 256),
            bf16(SIDES, 32, SLOT), bf16(SIDES, 32, SLOT),
            bf16(N_Z, TALL, 128), bf16(N_Z, TALL, 128), bf16(N_Z * TALL, 512),
            bf16(4, 128, 128), bf16(3, 128, 128), bf16(N_GRP, 128, 128),
            bf16(1, 128, 128), bf16(3, 128, 128), bf16(4, 128, 128),
            bf16(N_Z, TALL, 128), bf16(N_Z, 256, 128), f32(EARLY, NI, WIDE),
            dma((3 + 2 * CHUNKS,)),
            dma((CHUNKS, SIDES)), dma((CHUNKS, SIDES)), dma((CHUNKS, SIDES)), dma((CHUNKS, SIDES)),
            dma((SIDES,)), dma((SIDES,)),
            dma((7,)), dma((7,)), dma((3,)), dma((3,)), dma((7,)), dma((7,)),
            dma((3,)), dma((3,)), dma((3,)), dma((3,)), dma((7,)), dma((7,)),
        ],
        compiler_params=pltpu.CompilerParams(
            collective_id=0, has_side_effects=True, vmem_limit_bytes=LIMIT
        ),
        name="bddc_step",
    )(
        iterate, load, schur, local_inverse, basis, coarse_inverse, owner, shared_index,
        shared_count,
    )


def solution(mesh):
    rows = P(("grp", "sub"), None)
    placed = (rows, rows, rows, rows, rows, P("grp", None), rows, P(("grp", "sub"), None, None), rows)
    return jax.shard_map(
        on_device, mesh=mesh, in_specs=placed, out_specs=(rows, rows), check_vma=False
    )
```

time: 537 us -> 111 us (0.21); the launches traced: 529 us -> 109 us
  waiting for transfers between devices: 353 us -> 0 us
  Pallas kernels: 0 us -> 102 us
  other arithmetic: 62.9 us -> 0 us
  matrix products: 40.9 us -> 0 us
  starting transfers between devices: 27.8 us -> 0 us
  local copies, waits for them, and re-layouts: 29.7 us -> 6.48 us
  between operations: 14.5 us -> 0.64 us
    psum x1 -> x0, waiting for transfers between devices: 266 us -> none  [on_device(): coarse_residual = lax.psum(dense_terms, ('grp', 'sub'))]
    pallas_call x0 -> x1, Pallas kernels: none -> 102 us  [on_device(): pl.pallas_call(kernel, out_shape=(square, square), in_specs=[anywhere, an...]
    ppermute x12 -> x0, waiting for transfers between devices: 58.7 us -> none  [shifted(): return lax.ppermute(x, axis, [(i, (i + by) % size) for i in range(size)])]
    scatter-add x3 -> x0, other arithmetic: 47 us -> none  [the longest x2 36.1 us: add_incoming(): return values.astype(jnp.float32).at[flat_index].add(incoming.reshape(-1,...]
    dot_general x7 -> x0, matrix products: 40.9 us -> none  [the longest x1 9.64 us: on_device(): jnp.dot(coarse_inverse, coarse_residual, precision=highest, preferred_ele...]
    all_gather x1 -> x0, waiting for transfers between devices: 28.6 us -> none  [on_device(): coarse_values = lax.all_gather(block_values, 'grp', axis=0, tiled=True)]
    ppermute x12 -> x0, starting transfers between devices: 27.7 us -> none  [shifted(): return lax.ppermute(x, axis, [(i, (i + by) % size) for i in range(size)])]
    gather x2 -> x0, local copies, waits for them, and re-layouts: 15.2 us -> none  [outgoing(): rows = jnp.take(values, flat_index, axis=0)]
  transfers between devices with their start and end apart: 14 -> 0, of which waited for: 10 -> 0; matrix products, arithmetic and copies ran while one was open for 5% -> 0% of each run, Pallas kernels for 0% -> 0%
where the time goes in v2:
time: 111 us; the launch traced here: 109 us
  Pallas kernels  102 us (92%)
  local copies, waits for them, and re-layouts  6.48 us (6%)
    pallas_call x1, Pallas kernels, on_device(): pl.pallas_call(kernel, out_shape=(square, square), in_specs=[anywhere, an...  102 us
    unnamed x11, local copies, waits for them, and re-layouts  6.48 us

profile of v2, /device:TPU:1, one launch (start us, length us, event | category | flops | bytes accessed | tf_op | source)
XLA Modules:
  0.0 109.4 jit_solution(10764019927693104925)
XLA Ops:
  0.6 0.7 copy.11.idx_ref
  1.3 0.0 copy-start
  1.3 1.0 copy-done
  2.4 0.0 copy-start.1
  2.4 0.8 copy-done.1
  3.2 0.0 copy-start.2
  3.2 0.7 copy-done.2
  3.8 0.0 copy-start.3
  3.8 0.7 copy-done.3
  4.5 102.3 %bddc_step.1 = (bf16[1024,1024]{1,0:T(8,128)(2,1)S(1)}, bf16[1024,1024]{1,0:T(8,128)(2,1)S(1)}) custom-call(bf16[1024,1024]{1,0:T(8,128)(2,1)} %u_hbm.1, bf16[1024,1024]{1,0:T(8,128)(2,1)} %f_hbm.1, bf16[1024,1024]{1,0:T(8,128)(2,1)} %s_hbm.1, bf16[1024,1024]{1,0:T(8,128)(2,1)} %k_hbm.1, bf16[24,1024]{1,0:T(8,128)(2,1)S(1)} %copy-done.1, ...), custom_call_target="tpu_custom_call" | custom-call | tf_op jit(solution)/shard_map/bddc_step/pallas_call | solution.py:406
  106.8 1.3 %copy.14 = bf16[1024,1024]{1,0:T(8,128)(2,1)} copy(bf16[1024,1024]{1,0:T(8,128)(2,1)S(1)} %get-tuple-element.4) | data formatting | bytes 4194304
  108.1 1.3 %copy.15 = bf16[1024,1024]{1,0:T(8,128)(2,1)} copy(bf16[1024,1024]{1,0:T(8,128)(2,1)S(1)} %get-tuple-element.5) | data formatting | bytes 4194304
Async XLA Ops:
  1.3 1.0 copy-start
  2.4 0.8 copy-start.1
  3.2 0.7 copy-start.2
  3.8 0.7 copy-start.3

commit v3 on v2

--- a/solution.py
+++ b/solution.py
@@ -19,8 +19,9 @@
 N_Z = 8
 N_X = 4
 N_GRP = 8
+REL_BLOCKS = (0, 1, 4, 7)
 NCG = 1024
-LIMIT = 49 * 1024 * 1024
+LIMIT = 58 * 1024 * 1024
 EARLY = 2
 PER = WIDE // 128
 TALL = 176
@@ -50,10 +51,10 @@
     new_ref, res_ref,
     u, f, s, k, cinv, slots, pick, pick_t, wcol, wp,
     rb, cb, out1, in1, out2, in2,
-    owners, btr, bt, y_out, y_in, terms, terms_in, etr, t_out, t_in, pieces,
+    owners, btr, bt, y_out, y_in, terms, terms_in, etr, pieces,
     v_out, v_in, rel_val, own_val, near_val, early,
     load_sem, a1_send, a1_recv, a2_send, a2_recv, y_send, y_recv,
-    s1_send, s1_recv, s2_send, s2_recv, s3_send, s3_recv, s4_send, s4_recv,
+    s1_send, s1_recv, s3_send, s3_recv, s4_send, s4_recv,
     s5_send, s5_recv, s6_send, s6_recv,
 ):
     g = lax.axis_index("grp")
@@ -105,7 +106,7 @@
     slot_ids = lax.broadcasted_iota(jnp.int32, (1, CAP), 1)
     for j in range(SIDES):
         slots[j : j + 1, 0:CAP] = jnp.where(
-            slot_ids < cnt_ref[0, j], idx_ref[0, j : j + 1, :].astype(F32), -1.0
+            slot_ids < cnt_ref[0, j], idx_ref[j].astype(F32), -1.0
         )
     lane = lax.broadcasted_iota(jnp.int32, (SLOT, 128), 1).astype(F32)
     counts = [jnp.zeros((8, 128), F32)] * (NI // 128)
@@ -124,7 +125,8 @@
         loads[2 + 2 * c].wait()
         rest = (f[c].astype(F32) - dot(s[...], u[c])).astype(BF16)
         rb[c] = rest
-        out1[c] = dot(pick[...], rest).astype(BF16)
+        if c > 0:
+            out1[c] = dot(pick[...], rest).astype(BF16)
 
     def assembly_copy(out, into, send, recv, c, j):
         return remote(
@@ -144,8 +146,8 @@
             near(j),
         ).wait_recv()
 
-    def send_first(c):
-        for j in range(SIDES):
+    def send_first(c, sides=range(SIDES)):
+        for j in sides:
             assembly_copy(out1, in1, a1_send, a1_recv, c, j).start()
 
     def send_second(c, sides=range(SIDES)):
@@ -167,7 +169,11 @@
     pl.semaphore_wait(barrier, len(partners))
     for j in range(SIDES):
         remote(y_out.at[j], y_in.at[j ^ 1], y_send.at[j], y_recv.at[j ^ 1], near(j)).start()
-    send_first(0)
+    for j in range(SIDES):
+        rows = slice(SLOT * j, SLOT * (j + 1))
+        out1[0, rows, :] = dot(pick[rows, :], rb[0]).astype(BF16)
+        send_first(0, (j,))
+
 
     for c in range(1, CHUNKS):
         first(c)
@@ -258,44 +264,33 @@
         ]
         hot.append(jnp.zeros((8, 512), F32))
         etr[TALL * n : TALL * (n + 1), :] = jnp.concatenate(hot, axis=0).astype(BF16)
-    sums = dot_tn(etr[...], terms_in[...].reshape(N_Z * TALL, 128)).reshape(4, 128, 128)
-    t_out[...] = sums.astype(BF16)
-
-    def x_copy(d):
-        there = lax.rem(x + d, N_X)
-        return remote(
-            t_out.at[there], t_in.at[d - 1], s2_send.at[d - 1], s2_recv.at[d - 1], along_x(d)
-        )
-
-    for d in range(1, N_X):
-        x_copy(d).start()
-    second(0)
-    send_first(3)
-    for d in range(1, N_X):
-        x_copy(d).wait_recv()
-    own_block = t_out[x].astype(F32)
-    for d in range(1, N_X):
-        own_block += t_in[d - 1].astype(F32)
-    named = lax.rem(g + x + 2 * (x // 2) + 2 * (x // 3), N_GRP)
-    pieces[named] = own_block.astype(BF16)
+    sums = dot_tn(etr[...], terms_in[...].reshape(N_Z * TALL, 128))
+    pieces[g] = sums.astype(BF16).reshape(4, 128, 128)
 
     def g_copy(d):
         return remote(
-            pieces.at[named], pieces.at[named], s3_send.at[d - 1], s3_recv.at[d - 1], along_g(d)
+            pieces.at[g], pieces.at[g], s3_send.at[d - 1], s3_recv.at[d - 1], along_g(d)
         )
 
     for d in range(1, N_GRP):
         g_copy(d).start()
-    send_second(0)
+    send_first(3)
+    second(0)
+    send_second(0, range(3))
     second(1)
+    send_second(0, range(3, SIDES))
     for d in range(1, N_GRP):
-        here = lax.rem(named + N_GRP - d, N_GRP)
+        here = lax.rem(g + N_GRP - d, N_GRP)
         remote(
-            pieces.at[named], pieces.at[here], s3_send.at[d - 1], s3_recv.at[d - 1], along_g(d)
+            pieces.at[g], pieces.at[here], s3_send.at[d - 1], s3_recv.at[d - 1], along_g(d)
         ).wait_recv()
+    whole = [
+        sum(pieces[(n - r) % N_GRP, q].astype(F32) for q, r in enumerate(REL_BLOCKS))
+        for n in range(N_GRP)
+    ]
+    high, low = split(jnp.concatenate(whole, axis=0))
     chigh, clow = split(cinv[...])
-    flat = pieces[...].reshape(NI, 128)
-    partial = dot(chigh, flat) + dot(clow, flat)
+    partial = dot(chigh, high) + (dot(clow, high) + dot(chigh, low))
     v_out[0] = partial.astype(BF16)
 
     def v_copy(d):
@@ -305,9 +300,11 @@
 
     for d in range(1, N_X):
         v_copy(d).start()
+    second(2)
     send_second(1, range(3))
-    second(2)
+    second(3)
     send_second(1, range(3, SIDES))
+    send_second(2, range(3))
     for d in range(1, N_X):
         v_copy(d).wait_recv()
     solved = v_out[0].astype(F32)
@@ -323,8 +320,7 @@
 
     for n in range(1, 4):
         r_copy(n).start()
-    send_second(2)
-    second(3)
+    send_second(2, range(3, SIDES))
     for n in range(1, 4):
         r_copy(n).wait_recv()
     own_val[...] = dot(etr[...], rel_val[...].reshape(512, 128)).astype(BF16).reshape(N_Z, TALL, 128)
@@ -361,9 +357,12 @@
             total = early[c] + coarse
         else:
             total = u[c].astype(F32) + (cb[c].astype(F32) + coarse)
-            for j in range(SIDES):
-                assembly_wait(out2, in2, a2_send, a2_recv, c, j)
-            total += dot(pick_t[...], in2[c])
+            step = 2 if c == CHUNKS - 1 else SIDES
+            for low in range(0, SIDES, step):
+                for j in range(low, low + step):
+                    assembly_wait(out2, in2, a2_send, a2_recv, c, j)
+                rows = slice(SLOT * low, SLOT * (low + step))
+                total += dot(pick_t[:, rows], in2[c, rows, :])
         new_ref[:, c * WIDE : (c + 1) * WIDE] = total.astype(BF16)
 
     for c in range(CHUNKS):
@@ -380,7 +379,6 @@
         o_copy(d).wait_send()
         g_copy(d).wait_send()
     for d in range(1, N_X):
-        x_copy(d).wait_send()
         v_copy(d).wait_send()
     for n in range(1, 4):
         r_copy(n).wait_send()
@@ -392,7 +390,6 @@
     anywhere = pl.BlockSpec(memory_space=pltpu.HBM)
     vmem = pl.BlockSpec(memory_space=pltpu.VMEM)
     smem = pl.BlockSpec(memory_space=pltpu.SMEM)
-    square = jax.ShapeDtypeStruct((NI, NI), BF16)
     dma = pltpu.SemaphoreType.DMA
 
     def bf16(*shape):
@@ -403,9 +400,9 @@
 
     chunk = (CHUNKS, NI, WIDE)
     side = (CHUNKS, ROWS, WIDE)
-    return pl.pallas_call(
+    new, residual = pl.pallas_call(
         kernel,
-        out_shape=(square, square),
+        out_shape=(bf16(NI, NI), bf16(NI, NI)),
         in_specs=[anywhere, anywhere, anywhere, anywhere, vmem, anywhere, vmem, vmem, smem],
         out_specs=(vmem, vmem),
         scratch_shapes=[
@@ -415,13 +412,13 @@
             f32(16, 128), bf16(TALL, NI), bf16(NI, 256),
             bf16(SIDES, 32, SLOT), bf16(SIDES, 32, SLOT),
             bf16(N_Z, TALL, 128), bf16(N_Z, TALL, 128), bf16(N_Z * TALL, 512),
-            bf16(4, 128, 128), bf16(3, 128, 128), bf16(N_GRP, 128, 128),
+            bf16(N_GRP, 4, 128, 128),
             bf16(1, 128, 128), bf16(3, 128, 128), bf16(4, 128, 128),
             bf16(N_Z, TALL, 128), bf16(N_Z, 256, 128), f32(EARLY, NI, WIDE),
             dma((3 + 2 * CHUNKS,)),
             dma((CHUNKS, SIDES)), dma((CHUNKS, SIDES)), dma((CHUNKS, SIDES)), dma((CHUNKS, SIDES)),
             dma((SIDES,)), dma((SIDES,)),
-            dma((7,)), dma((7,)), dma((3,)), dma((3,)), dma((7,)), dma((7,)),
+            dma((7,)), dma((7,)), dma((7,)), dma((7,)),
             dma((3,)), dma((3,)), dma((3,)), dma((3,)), dma((7,)), dma((7,)),
         ],
         compiler_params=pltpu.CompilerParams(
@@ -429,9 +426,10 @@
         ),
         name="bddc_step",
     )(
-        iterate, load, schur, local_inverse, basis, coarse_inverse, owner, shared_index,
-        shared_count,
+        iterate, load, schur, local_inverse, basis, coarse_inverse, owner,
+        jnp.transpose(shared_index, (1, 0, 2)), shared_count,
     )
+    return new, residual
 
 
 def solution(mesh):

time: 111 us -> 105 us (0.946)
  the two profiles are of different devices: /device:TPU:1 before, /device:TPU:122 now
where the time goes in v3:
time: 105 us
  Pallas kernels  102 us (97%)
  local copies, waits for them, and re-layouts  2.64 us (3%)
    pallas_call x1, Pallas kernels, on_device(): pl.pallas_call(kernel, out_shape=(bf16(NI, NI), bf16(NI, NI)), in_specs=[...  102 us
    unnamed x2, local copies, waits for them, and re-layouts  2.64 us

profile of v3, /device:TPU:122, one launch (start us, length us, event | category | flops | bytes accessed | tf_op | source)
XLA Modules:
  0.0 104.9 jit_solution(11730305183765277713)
XLA Ops:
  0.6 101.6 %bddc_step.1 = (bf16[1024,1024]{1,0:T(8,128)(2,1)S(1)}, bf16[1024,1024]{1,0:T(8,128)(2,1)S(1)}) custom-call(bf16[1024,1024]{1,0:T(8,128)(2,1)} %u_hbm.1, bf16[1024,1024]{1,0:T(8,128)(2,1)} %f_hbm.1, bf16[1024,1024]{1,0:T(8,128)(2,1)} %s_hbm.1, bf16[1024,1024]{1,0:T(8,128)(2,1)} %k_hbm.1, bf16[24,1024]{1,0:T(8,128)(2,1)} %p_ref.1, f32[128,1024]{1,0:T(8,128)} %cinv_hbm.1, ...), custom_call_target="tpu_custom_call" | custom-call | tf_op jit(solution)/shard_map/bddc_step/pallas_call | solution.py:403
  102.3 1.3 %copy.13 = bf16[1024,1024]{1,0:T(8,128)(2,1)} copy(bf16[1024,1024]{1,0:T(8,128)(2,1)S(1)} %get-tuple-element.2) | data formatting | bytes 4194304
  103.6 1.3 %copy.14 = bf16[1024,1024]{1,0:T(8,128)(2,1)} copy(bf16[1024,1024]{1,0:T(8,128)(2,1)S(1)} %get-tuple-element.3) | data formatting | bytes 4194304

commit v4 on v3

--- a/solution.py
+++ b/solution.py
@@ -301,10 +301,9 @@
     for d in range(1, N_X):
         v_copy(d).start()
     second(2)
-    send_second(1, range(3))
+    send_second(1)
     second(3)
-    send_second(1, range(3, SIDES))
-    send_second(2, range(3))
+    send_second(2)
     for d in range(1, N_X):
         v_copy(d).wait_recv()
     solved = v_out[0].astype(F32)
@@ -320,7 +319,7 @@
 
     for n in range(1, 4):
         r_copy(n).start()
-    send_second(2, range(3, SIDES))
+    send_second(3, range(3))
     for n in range(1, 4):
         r_copy(n).wait_recv()
     own_val[...] = dot(etr[...], rel_val[...].reshape(512, 128)).astype(BF16).reshape(N_Z, TALL, 128)
@@ -334,7 +333,7 @@
 
     for d in range(1, N_Z):
         o_copy(d).start()
-    send_second(3)
+    send_second(3, range(3, SIDES))
     near_val[z, pl.ds(0, TALL)] = own_val[z]
 
     def second_sum(c):

time: 105 us -> 105 us (level)
  the two profiles are of different devices: /device:TPU:122 before, /device:TPU:1 now
where the time goes in v4:
time: 105 us; the launch traced here: 104 us
  Pallas kernels  100 us (95%)
  local copies, waits for them, and re-layouts  2.64 us (3%)
    pallas_call x1, Pallas kernels, on_device(): pl.pallas_call(kernel, out_shape=(bf16(NI, NI), bf16(NI, NI)), in_specs=[...  100 us
    unnamed x2, local copies, waits for them, and re-layouts  2.64 us

profile of v4, /device:TPU:1, one launch (start us, length us, event | category | flops | bytes accessed | tf_op | source)
XLA Modules:
  0.0 103.7 jit_solution(9766762637549842939)
XLA Ops:
  0.6 100.4 %bddc_step.1 = (bf16[1024,1024]{1,0:T(8,128)(2,1)S(1)}, bf16[1024,1024]{1,0:T(8,128)(2,1)S(1)}) custom-call(bf16[1024,1024]{1,0:T(8,128)(2,1)} %u_hbm.1, bf16[1024,1024]{1,0:T(8,128)(2,1)} %f_hbm.1, bf16[1024,1024]{1,0:T(8,128)(2,1)} %s_hbm.1, bf16[1024,1024]{1,0:T(8,128)(2,1)} %k_hbm.1, bf16[24,1024]{1,0:T(8,128)(2,1)} %p_ref.1, f32[128,1024]{1,0:T(8,128)} %cinv_hbm.1, ...), custom_call_target="tpu_custom_call" | custom-call | tf_op jit(solution)/shard_map/bddc_step/pallas_call | solution.py:402
  101.0 1.3 %copy.13 = bf16[1024,1024]{1,0:T(8,128)(2,1)} copy(bf16[1024,1024]{1,0:T(8,128)(2,1)S(1)} %get-tuple-element.2) | data formatting | bytes 4194304
  102.4 1.3 %copy.14 = bf16[1024,1024]{1,0:T(8,128)(2,1)} copy(bf16[1024,1024]{1,0:T(8,128)(2,1)S(1)} %get-tuple-element.3) | data formatting | bytes 4194304
